TPU v7x, 512 devices: a whole 4x4x16 slice. The times are simulated.
512 devices in a mesh: chan: 64 (over y, x, z_hi, core), freq: 8 (over z_lo).
Axes of the slice: x: 4, y: 4, z: 16 (z_hi: 2, z_lo: 8; z = z_hi * 8 + z_lo), core: 2. Of those that a mesh axis runs over, the one named last changes fastest.
Arguments:
- spectra: bfloat16 [256, 2, 16, 8192], P('freq', None, None, 'chan'), may hold values from -20 to 20
- model: bfloat16 [256, 2, 8, 8192], P('freq', None, None, 'chan'), may hold values from -6 to 6
- channel_ok: int32 [8192], replicated, may hold values 0 or 1
- limits: int32 [64], replicated, may hold values from 128 to 1024, as said below
Outputs:
- adjoint: float32 [256, 2, 16, 8192], P('freq', None, None, 'chan')
- misfit: float32 [], replicated
Inputs may be any that keep to these rules, and one draw needn't show every extreme that they name: `limits`: one block has the limit 128 and another the limit 1024.
All inputs are finite; a program needn't handle non-finite values.
Results may differ from a plain program's by a relative error of at most 0.00053.
Values may be sent and summed in bfloat16 or wider, within the bound.
A program may use at most 64 MiB of HBM per device.

v0:
```python
import jax
import jax.numpy as jnp
from jax import lax
from jax.sharding import PartitionSpec as P

F = 256
W = 16
BAND = 1024


def shifted(x, axis, by):
    peers = lax.axis_size(axis)
    return lax.ppermute(x, axis, [(i, (i + by) % peers) for i in range(peers)])


def pair_terms(first_block, second_block, ok_first, ok_second, limit_first, shift_blocks):
    bin_count = first_block.shape[0]
    row_count = first_block.shape[2]
    block_width = first_block.shape[3]
    row_scale = jnp.concatenate(
        [jnp.full((W,), 1.0 / W, jnp.float32), jnp.full((row_count - W,), -1.0, jnp.float32)]
    ).astype(jnp.bfloat16)
    scaled = first_block * row_scale[None, None, :, None]
    stacked_left = jnp.stack(
        [
            scaled.reshape(bin_count, 2 * row_count, block_width),
            jnp.concatenate([scaled[:, 1], -scaled[:, 0]], axis=1),
        ],
        axis=0,
    )
    right_rows = second_block.reshape(bin_count, 2 * row_count, block_width)
    cross_spec = jnp.einsum(
        "xfrc,frd->xfcd", stacked_left, right_rows, preferred_element_type=jnp.float32
    )
    row_index = lax.broadcasted_iota(jnp.int32, (block_width, block_width), 0)
    col_index = lax.broadcasted_iota(jnp.int32, (block_width, block_width), 1)
    offset = shift_blocks * block_width + col_index - row_index
    inside = ((offset >= 1) & (offset <= limit_first)).astype(jnp.float32)
    live_mask = ok_first[:, None] * ok_second[None, :] * inside
    residual = cross_spec * live_mask[None, None]
    piece_loss = 0.5 * jnp.sum(residual * residual)
    rounded = residual.astype(jnp.bfloat16)
    far_spec = second_block[:, :, :W].reshape(bin_count, 2 * W, block_width)
    near_spec = first_block[:, :, :W].reshape(bin_count, 2 * W, block_width)
    toward = jnp.einsum("xfcd,fvd->xfvc", rounded, far_spec, preferred_element_type=jnp.float32)
    first_real = toward[0, :, :W] - toward[1, :, W:]
    first_imag = toward[0, :, W:] + toward[1, :, :W]
    backward = jnp.einsum("xfcd,fvc->xfvd", rounded, near_spec, preferred_element_type=jnp.float32)
    second_real = backward[0, :, :W] + backward[1, :, W:]
    second_imag = backward[0, :, W:] - backward[1, :, :W]
    return (
        piece_loss,
        jnp.stack([first_real, first_imag], axis=1),
        jnp.stack([second_real, second_imag], axis=1),
    )


def shards(spectra, model, channel_ok, limits):
    payload = jnp.concatenate([spectra, model], axis=2)
    block_width = spectra.shape[3]
    band_blocks = BAND // block_width
    block_total = lax.axis_size("chan")
    block_index = lax.axis_index("chan")
    ok_all = channel_ok.astype(jnp.float32)

    def flags_of(move):
        start = (block_index + move) % block_total * block_width
        return lax.dynamic_slice_in_dim(ok_all, start, block_width)

    ok_own = flags_of(0)
    limit_own = lax.dynamic_index_in_dim(limits, block_index % block_total, keepdims=False)
    misfit_sum, near_terms, far_terms = pair_terms(payload, payload, ok_own, ok_own, limit_own, 0)
    adjoint_acc = near_terms + far_terms
    for s in range(1, band_blocks + 1):
        ahead_block = shifted(payload, "chan", -s)
        piece_loss, near_terms, far_terms = pair_terms(
            payload, ahead_block, ok_own, flags_of(s), limit_own, s
        )
        misfit_sum = misfit_sum + piece_loss
        adjoint_acc = adjoint_acc + near_terms
        adjoint_acc = adjoint_acc + shifted(far_terms, "chan", s)
    misfit_total = lax.psum(misfit_sum, ("chan", "freq"))
    misfit = misfit_total / float(F * block_width * block_total * BAND)
    return (adjoint_acc * (1.0 / W), misfit)


def solution(mesh):
    return jax.shard_map(
        shards,
        mesh=mesh,
        in_specs=(P("freq", None, None, "chan"), P("freq", None, None, "chan"), P(), P()),
        out_specs=(P("freq", None, None, "chan"), P()),
        check_vma=False,
    )
```

profile of v0, /device:TPU:104, one launch (start us, length us, event | category | flops | bytes accessed | tf_op | source)
XLA Modules:
  0.0 482.6 jit_solution(15571919331790536662)
XLA Ops:
  0.7 1.0 constant_dynamic-update-slice_fusion.1
  1.6 0.9 constant_dynamic-update-slice_fusion
  2.6 1.5 broadcast_multiply_fusion
  4.0 4.8 collective-permute-start.14
  8.8 1.9 collective-permute-start.12
  10.8 17.6 %collective-permute-start.10 = (bf16[32,2,24,128]{3,2,0,1:T(8,128)(2,1)}, bf16[32,2,24,128]{3,2,0,1:T(8,128)(2,1)S(1)}, u32[]{:S(2)}, u32[]{:S(2)}) collective-permute-start(bf16[32,2,24,128]{3,2,0,1:T(8,128)(2,1)} %get-tuple-element.61), channel_id=1, source_target_pairs={{0,464},{8,472},{16,480},{24,488},{32,496},{40,504},{48,0},{56,8},... | collective-permute-start | bytes 1179656 | tf_op jit(solution)/shard_map/ppermute | solution.py:13
  28.4 12.3 %collective-permute-start.8 = (bf16[32,2,24,128]{3,2,0,1:T(8,128)(2,1)}, bf16[32,2,24,128]{3,2,0,1:T(8,128)(2,1)S(1)}, u32[]{:S(2)}, u32[]{:S(2)}) collective-permute-start(bf16[32,2,24,128]{3,2,0,1:T(8,128)(2,1)} %get-tuple-element.61), channel_id=1, source_target_pairs={{0,472},{8,480},{16,488},{24,496},{32,504},{40,0},{48,8},{56,16},{... | collective-permute-start | bytes 1179656 | tf_op jit(solution)/shard_map/ppermute | solution.py:13
  40.7 3.0 collective-permute-start.6
  45.0 1.0 multiply_select_fusion.8
  46.0 1.9 multiply_reduce_fusion.8
  47.9 0.8 fusion.91
  49.2 0.8 fusion.144
  50.0 1.9 collective-permute-start.4
  51.9 1.9 multiply_reduce_fusion
  53.8 0.8 fusion.88
  55.2 0.8 fusion.114
  56.0 1.9 collective-permute-start.2
  57.9 2.0 multiply_reduce_fusion.1
  59.9 0.8 fusion.82
  61.2 0.9 fusion.118
  62.1 56.0 %collective-permute-start = (bf16[32,2,24,128]{3,2,0,1:T(8,128)(2,1)}, bf16[32,2,24,128]{3,2,0,1:T(8,128)(2,1)S(1)}, u32[]{:S(2)}, u32[]{:S(2)}) collective-permute-start(bf16[32,2,24,128]{3,2,0,1:T(8,128)(2,1)} %get-tuple-element.61), channel_id=1, source_target_pairs={{0,504},{8,0},{16,8},{24,16},{32,24},{40,32},{48,40},{56,48},{64,5... | collective-permute-start | bytes 1179656 | tf_op jit(solution)/shard_map/ppermute | solution.py:13
  118.2 2.0 multiply_reduce_fusion.2
  120.1 0.8 fusion.76
  121.5 0.8 pad_maximum_fusion.8
  122.3 0.9 fusion.122
  123.2 12.3 %collective-permute-start.15 = (f32[32,2,16,128]{3,2,0,1:T(8,128)}, f32[32,2,16,128]{3,2,0,1:T(8,128)}, u32[]{:S(2)}, u32[]{:S(2)}) collective-permute-start(f32[32,2,16,128]{3,2,0,1:T(8,128)} %pad_maximum_fusion.8), channel_id=1, source_target_pairs={{0,64},{8,72},{16,80},{24,88},{32,96},{40,104},{48,112},{56,120},{... | collective-permute-start | bytes 1572872 | tf_op jit(solution)/shard_map/ppermute | solution.py:13
  135.6 2.0 multiply_reduce_fusion.3
  137.6 0.8 fusion.70
  138.9 0.9 pad_maximum_fusion.7
  139.8 0.9 fusion.126
  140.7 1.9 collective-permute-start.13
  142.6 2.0 multiply_reduce_fusion.4
  144.6 0.8 fusion.64
  145.9 0.8 pad_maximum_fusion.6
  146.8 0.9 fusion.130
  147.7 1.9 collective-permute-start.11
  149.6 1.9 multiply_reduce_fusion.5
  151.6 0.8 fusion.58
  152.4 0.9 fusion.132
  153.3 0.9 pad_maximum_fusion.5
  154.6 6.8 %collective-permute-start.9 = (f32[32,2,16,128]{3,2,0,1:T(8,128)}, f32[32,2,16,128]{3,2,0,1:T(8,128)}, u32[]{:S(2)}, u32[]{:S(2)}) collective-permute-start(f32[32,2,16,128]{3,2,0,1:T(8,128)} %pad_maximum_fusion.5), channel_id=1, source_target_pairs={{0,40},{8,48},{16,56},{24,64},{32,72},{40,80},{48,88},{56,96},{64,... | collective-permute-start | bytes 1572872 | tf_op jit(solution)/shard_map/ppermute | solution.py:13
  161.5 1.9 multiply_reduce_fusion.6
  163.4 0.8 fusion.52
  164.2 0.9 fusion.134
  165.1 0.7 copy.62
  165.8 0.8 pad_maximum_fusion.4
  166.6 0.9 fusion.136
  167.5 19.7 %collective-permute-start.7 = (f32[32,2,16,128]{3,2,0,1:T(8,128)}, f32[32,2,16,128]{3,2,0,1:T(8,128)}, u32[]{:S(2)}, u32[]{:S(2)}) collective-permute-start(f32[32,2,16,128]{3,2,0,1:T(8,128)} %pad_maximum_fusion.4), channel_id=1, source_target_pairs={{0,32},{8,40},{16,48},{24,56},{32,64},{40,72},{48,80},{56,88},{64,... | collective-permute-start | bytes 1572872 | tf_op jit(solution)/shard_map/ppermute | solution.py:13
  187.3 2.0 multiply_reduce_fusion.7
  189.2 0.8 fusion.46
  190.0 0.9 fusion.140
  197.4 166.3 %psum.7 = f32[]{:T(128)} all-reduce(f32[]{:T(128)S(6)} %add.578), channel_id=1, replica_groups=mesh['chan'=64,'freq'=8] {'chan','freq'}, use_global_device_ids=true, to_apply=%region_9.10 | all-reduce | flops 1 | bytes 8 | tf_op jit(solution)/shard_map/psum | solution.py:82
  363.7 1.9 pad_maximum_fusion.3
  365.6 1.9 pad_maximum_fusion.2
  367.5 0.9 pad_maximum_fusion.1
  369.1 1.5 fusion.49
  370.7 8.0 %collective-permute-start.5 = (f32[32,2,16,128]{3,2,0,1:T(8,128)S(1)}, f32[32,2,16,128]{3,2,0,1:T(8,128)S(1)}, u32[]{:S(2)}, u32[]{:S(2)}) collective-permute-start(f32[32,2,16,128]{3,2,0,1:T(8,128)S(1)} %copy-done.18), channel_id=1, source_target_pairs={{0,24},{8,32},{16,40},{24,48},{32,56},{40,64},{48,72},{56,80},{64,... | collective-permute-start | bytes 1572872 | tf_op jit(solution)/shard_map/ppermute | solution.py:13
  378.7 4.5 collective-permute-start.3
  383.2 1.9 collective-permute-start.1
  385.8 37.9 %collective-permute-done.5 = f32[32,2,16,128]{3,2,0,1:T(8,128)S(1)} collective-permute-done((f32[32,2,16,128]{3,2,0,1:T(8,128)S(1)}, f32[32,2,16,128]{3,2,0,1:T(8,128)S(1)}, u32[]{:S(2)}, u32[]{:S(2)}) %collective-permute-start.5) | collective-permute-done | bytes 524320 | tf_op jit(solution)/shard_map/ppermute | solution.py:13
  423.7 48.4 %collective-permute-done.3 = f32[32,2,16,128]{3,2,0,1:T(8,128)S(1)} collective-permute-done((f32[32,2,16,128]{3,2,0,1:T(8,128)S(1)}, f32[32,2,16,128]{3,2,0,1:T(8,128)S(1)}, u32[]{:S(2)}, u32[]{:S(2)}) %collective-permute-start.3) | collective-permute-done | bytes 524320 | tf_op jit(solution)/shard_map/ppermute | solution.py:13
  472.2 6.0 %collective-permute-done.1 = f32[32,2,16,128]{3,2,0,1:T(8,128)S(1)} collective-permute-done((f32[32,2,16,128]{3,2,0,1:T(8,128)S(1)}, f32[32,2,16,128]{3,2,0,1:T(8,128)S(1)}, u32[]{:S(2)}, u32[]{:S(2)}) %collective-permute-start.1) | collective-permute-done | bytes 524320 | tf_op jit(solution)/shard_map/ppermute | solution.py:13
  478.3 2.3 fusion.110
  480.6 0.9 copy.104
  (113 shorter events, 6.4 us)
Async XLA Ops:
  0.6 43.4 %copy-start.22 = (bf16[24]{0:T(256)(128)(2,1)S(1)}, bf16[24]{0:T(256)(128)(2,1)}, u32[]{:S(2)}) copy-start(bf16[24]{0:T(256)(128)(2,1)} %constant.88.clone.1) | copy-start | bytes 148
  0.6 43.3 %copy-start.21 = (s32[8192]{0:T(1024)S(1)}, s32[8192]{0:T(1024)}, u32[]{:S(2)}) copy-start(s32[8192]{0:T(1024)} %param.6) | copy-start | bytes 98308
  0.7 43.5 %copy-start.23 = (s32[64]{0:T(128)S(1)}, s32[64]{0:T(128)}, u32[]{:S(2)}) copy-start(s32[64]{0:T(128)} %param.7) | copy-start | bytes 772
  4.0 45.9 %collective-permute-start.14 = (bf16[32,2,24,128]{3,2,0,1:T(8,128)(2,1)}, bf16[32,2,24,128]{3,2,0,1:T(8,128)(2,1)S(1)}, u32[]{:S(2)}, u32[]{:S(2)}) collective-permute-start(bf16[32,2,24,128]{3,2,0,1:T(8,128)(2,1)} %get-tuple-element.61), channel_id=1, source_target_pairs={{0,448},{8,456},{16,464},{24,472},{32,480},{40,488},{48,496},{56,5... | collective-permute-start | bytes 1179656 | tf_op jit(solution)/shard_map/ppermute | solution.py:13
  8.8 47.1 %collective-permute-start.12 = (bf16[32,2,24,128]{3,2,0,1:T(8,128)(2,1)}, bf16[32,2,24,128]{3,2,0,1:T(8,128)(2,1)S(1)}, u32[]{:S(2)}, u32[]{:S(2)}) collective-permute-start(bf16[32,2,24,128]{3,2,0,1:T(8,128)(2,1)} %get-tuple-element.61), channel_id=1, source_target_pairs={{0,456},{8,464},{16,472},{24,480},{32,488},{40,496},{48,504},{56,0... | collective-permute-start | bytes 1179656 | tf_op jit(solution)/shard_map/ppermute | solution.py:13
  10.8 51.3 %collective-permute-start.10 = (bf16[32,2,24,128]{3,2,0,1:T(8,128)(2,1)}, bf16[32,2,24,128]{3,2,0,1:T(8,128)(2,1)S(1)}, u32[]{:S(2)}, u32[]{:S(2)}) collective-permute-start(bf16[32,2,24,128]{3,2,0,1:T(8,128)(2,1)} %get-tuple-element.61), channel_id=1, source_target_pairs={{0,464},{8,472},{16,480},{24,488},{32,496},{40,504},{48,0},{56,8},... | collective-permute-start | bytes 1179656 | tf_op jit(solution)/shard_map/ppermute | solution.py:13
  28.4 94.8 %collective-permute-start.8 = (bf16[32,2,24,128]{3,2,0,1:T(8,128)(2,1)}, bf16[32,2,24,128]{3,2,0,1:T(8,128)(2,1)S(1)}, u32[]{:S(2)}, u32[]{:S(2)}) collective-permute-start(bf16[32,2,24,128]{3,2,0,1:T(8,128)(2,1)} %get-tuple-element.61), channel_id=1, source_target_pairs={{0,472},{8,480},{16,488},{24,496},{32,504},{40,0},{48,8},{56,16},{... | collective-permute-start | bytes 1179656 | tf_op jit(solution)/shard_map/ppermute | solution.py:13
  40.7 100.0 %collective-permute-start.6 = (bf16[32,2,24,128]{3,2,0,1:T(8,128)(2,1)}, bf16[32,2,24,128]{3,2,0,1:T(8,128)(2,1)S(1)}, u32[]{:S(2)}, u32[]{:S(2)}) collective-permute-start(bf16[32,2,24,128]{3,2,0,1:T(8,128)(2,1)} %get-tuple-element.61), channel_id=1, source_target_pairs={{0,480},{8,488},{16,496},{24,504},{32,0},{40,8},{48,16},{56,24},{6... | collective-permute-start | bytes 1179656 | tf_op jit(solution)/shard_map/ppermute | solution.py:13
  46.0 1.9 copy-start
  50.0 97.7 %collective-permute-start.4 = (bf16[32,2,24,128]{3,2,0,1:T(8,128)(2,1)}, bf16[32,2,24,128]{3,2,0,1:T(8,128)(2,1)S(1)}, u32[]{:S(2)}, u32[]{:S(2)}) collective-permute-start(bf16[32,2,24,128]{3,2,0,1:T(8,128)(2,1)} %get-tuple-element.61), channel_id=1, source_target_pairs={{0,488},{8,496},{16,504},{24,0},{32,8},{40,16},{48,24},{56,32},{64... | collective-permute-start | bytes 1179656 | tf_op jit(solution)/shard_map/ppermute | solution.py:13
  56.0 98.6 %collective-permute-start.2 = (bf16[32,2,24,128]{3,2,0,1:T(8,128)(2,1)}, bf16[32,2,24,128]{3,2,0,1:T(8,128)(2,1)S(1)}, u32[]{:S(2)}, u32[]{:S(2)}) collective-permute-start(bf16[32,2,24,128]{3,2,0,1:T(8,128)(2,1)} %get-tuple-element.61), channel_id=1, source_target_pairs={{0,496},{8,504},{16,0},{24,8},{32,16},{40,24},{48,32},{56,40},{64,... | collective-permute-start | bytes 1179656 | tf_op jit(solution)/shard_map/ppermute | solution.py:13
  62.1 105.4 %collective-permute-start = (bf16[32,2,24,128]{3,2,0,1:T(8,128)(2,1)}, bf16[32,2,24,128]{3,2,0,1:T(8,128)(2,1)S(1)}, u32[]{:S(2)}, u32[]{:S(2)}) collective-permute-start(bf16[32,2,24,128]{3,2,0,1:T(8,128)(2,1)} %get-tuple-element.61), channel_id=1, source_target_pairs={{0,504},{8,0},{16,8},{24,16},{32,24},{40,32},{48,40},{56,48},{64,5... | collective-permute-start | bytes 1179656 | tf_op jit(solution)/shard_map/ppermute | solution.py:13
  123.2 247.5 %collective-permute-start.15 = (f32[32,2,16,128]{3,2,0,1:T(8,128)}, f32[32,2,16,128]{3,2,0,1:T(8,128)}, u32[]{:S(2)}, u32[]{:S(2)}) collective-permute-start(f32[32,2,16,128]{3,2,0,1:T(8,128)} %pad_maximum_fusion.8), channel_id=1, source_target_pairs={{0,64},{8,72},{16,80},{24,88},{32,96},{40,104},{48,112},{56,120},{... | collective-permute-start | bytes 1572872 | tf_op jit(solution)/shard_map/ppermute | solution.py:13
  140.7 238.0 %collective-permute-start.13 = (f32[32,2,16,128]{3,2,0,1:T(8,128)}, f32[32,2,16,128]{3,2,0,1:T(8,128)}, u32[]{:S(2)}, u32[]{:S(2)}) collective-permute-start(f32[32,2,16,128]{3,2,0,1:T(8,128)} %pad_maximum_fusion.7), channel_id=1, source_target_pairs={{0,56},{8,64},{16,72},{24,80},{32,88},{40,96},{48,104},{56,112},{6... | collective-permute-start | bytes 1572872 | tf_op jit(solution)/shard_map/ppermute | solution.py:13
  147.7 235.5 %collective-permute-start.11 = (f32[32,2,16,128]{3,2,0,1:T(8,128)}, f32[32,2,16,128]{3,2,0,1:T(8,128)}, u32[]{:S(2)}, u32[]{:S(2)}) collective-permute-start(f32[32,2,16,128]{3,2,0,1:T(8,128)} %pad_maximum_fusion.6), channel_id=1, source_target_pairs={{0,48},{8,56},{16,64},{24,72},{32,80},{40,88},{48,96},{56,104},{64... | collective-permute-start | bytes 1572872 | tf_op jit(solution)/shard_map/ppermute | solution.py:13
  154.6 231.2 %collective-permute-start.9 = (f32[32,2,16,128]{3,2,0,1:T(8,128)}, f32[32,2,16,128]{3,2,0,1:T(8,128)}, u32[]{:S(2)}, u32[]{:S(2)}) collective-permute-start(f32[32,2,16,128]{3,2,0,1:T(8,128)} %pad_maximum_fusion.5), channel_id=1, source_target_pairs={{0,40},{8,48},{16,56},{24,64},{32,72},{40,80},{48,88},{56,96},{64,... | collective-permute-start | bytes 1572872 | tf_op jit(solution)/shard_map/ppermute | solution.py:13
  167.5 218.3 %collective-permute-start.7 = (f32[32,2,16,128]{3,2,0,1:T(8,128)}, f32[32,2,16,128]{3,2,0,1:T(8,128)}, u32[]{:S(2)}, u32[]{:S(2)}) collective-permute-start(f32[32,2,16,128]{3,2,0,1:T(8,128)} %pad_maximum_fusion.4), channel_id=1, source_target_pairs={{0,32},{8,40},{16,48},{24,56},{32,64},{40,72},{48,80},{56,88},{64,... | collective-permute-start | bytes 1572872 | tf_op jit(solution)/shard_map/ppermute | solution.py:13
  189.2 1.7 copy-start.1
  196.7 170.8 %copy-start.15 = (f32[32,1,16,128]{3,2,0,1:T(8,128)S(1)}, f32[32,1,16,128]{3,2,0,1:T(8,128)}, u32[]{:S(2)}) copy-start(f32[32,1,16,128]{3,2,0,1:T(8,128)} %get-tuple-element.28) | copy-start | bytes 786436
  363.7 3.8 copy-start.16
  369.0 1.6 copy-start.18
  369.0 9.7 %copy-start.19 = (f32[32,2,16,128]{3,2,0,1:T(8,128)S(1)}, f32[32,2,16,128]{3,2,0,1:T(8,128)}, u32[]{:S(2)}) copy-start(f32[32,2,16,128]{3,2,0,1:T(8,128)} %pad_maximum_fusion.2) | copy-start | bytes 1572868
  369.0 14.2 %copy-start.20 = (f32[32,2,16,128]{3,2,0,1:T(8,128)S(1)}, f32[32,2,16,128]{3,2,0,1:T(8,128)}, u32[]{:S(2)}) copy-start(f32[32,2,16,128]{3,2,0,1:T(8,128)} %pad_maximum_fusion.1) | copy-start | bytes 1572868
  369.1 16.1 %copy-start.2 = (bf16[2,32,128,128]{2,3,0,1:T(8,128)(2,1)S(1)}, bf16[2,32,128,128]{2,3,0,1:T(8,128)(2,1)}, u32[]{:S(2)}) copy-start(bf16[2,32,128,128]{2,3,0,1:T(8,128)(2,1)} %copy-done.1) | copy-start | bytes 6291460
  369.1 16.1 %copy-start.17 = (bf16[32,2,16,128]{3,2,1,0:T(8,128)(2,1)S(1)}, bf16[32,2,16,128]{3,2,1,0:T(8,128)(2,1)}, u32[]{:S(2)}) copy-start(bf16[32,2,16,128]{3,2,1,0:T(8,128)(2,1)} %copy.56) | copy-start | bytes 786436
  370.7 53.0 %collective-permute-start.5 = (f32[32,2,16,128]{3,2,0,1:T(8,128)S(1)}, f32[32,2,16,128]{3,2,0,1:T(8,128)S(1)}, u32[]{:S(2)}, u32[]{:S(2)}) collective-permute-start(f32[32,2,16,128]{3,2,0,1:T(8,128)S(1)} %copy-done.18), channel_id=1, source_target_pairs={{0,24},{8,32},{16,40},{24,48},{32,56},{40,64},{48,72},{56,80},{64,... | collective-permute-start | bytes 1572872 | tf_op jit(solution)/shard_map/ppermute | solution.py:13
  378.7 93.5 %collective-permute-start.3 = (f32[32,2,16,128]{3,2,0,1:T(8,128)S(1)}, f32[32,2,16,128]{3,2,0,1:T(8,128)S(1)}, u32[]{:S(2)}, u32[]{:S(2)}) collective-permute-start(f32[32,2,16,128]{3,2,0,1:T(8,128)S(1)} %copy-done.19), channel_id=1, source_target_pairs={{0,16},{8,24},{16,32},{24,40},{32,48},{40,56},{48,64},{56,72},{64,... | collective-permute-start | bytes 1572872 | tf_op jit(solution)/shard_map/ppermute | solution.py:13
  383.2 95.0 %collective-permute-start.1 = (f32[32,2,16,128]{3,2,0,1:T(8,128)S(1)}, f32[32,2,16,128]{3,2,0,1:T(8,128)S(1)}, u32[]{:S(2)}, u32[]{:S(2)}) collective-permute-start(f32[32,2,16,128]{3,2,0,1:T(8,128)S(1)} %copy-done.20), channel_id=1, source_target_pairs={{0,8},{8,16},{16,24},{24,32},{32,40},{40,48},{48,56},{56,64},{64,7... | collective-permute-start | bytes 1572872 | tf_op jit(solution)/shard_map/ppermute | solution.py:13
  385.2 93.0 %copy-start.3 = (f32[32,1,16,128]{3,2,0,1:T(8,128)S(1)}, f32[32,1,16,128]{3,2,0,1:T(8,128)}, u32[]{:S(2)}) copy-start(f32[32,1,16,128]{3,2,0,1:T(8,128)} %get-tuple-element.25) | copy-start | bytes 786436
  385.2 93.0 %copy-start.4 = (f32[32,1,16,128]{3,2,0,1:T(8,128)S(1)}, f32[32,1,16,128]{3,2,0,1:T(8,128)}, u32[]{:S(2)}) copy-start(f32[32,1,16,128]{3,2,0,1:T(8,128)} %get-tuple-element.55) | copy-start | bytes 786436
  385.2 93.0 %copy-start.5 = (f32[32,1,16,128]{3,2,0,1:T(8,128)S(1)}, f32[32,1,16,128]{3,2,0,1:T(8,128)}, u32[]{:S(2)}) copy-start(f32[32,1,16,128]{3,2,0,1:T(8,128)} %get-tuple-element.50) | copy-start | bytes 786436
  385.2 93.0 %copy-start.6 = (f32[32,1,16,128]{3,2,0,1:T(8,128)S(1)}, f32[32,1,16,128]{3,2,0,1:T(8,128)}, u32[]{:S(2)}) copy-start(f32[32,1,16,128]{3,2,0,1:T(8,128)} %get-tuple-element.51) | copy-start | bytes 786436
  385.2 93.0 %copy-start.7 = (f32[32,1,16,128]{3,2,0,1:T(8,128)S(1)}, f32[32,1,16,128]{3,2,0,1:T(8,128)}, u32[]{:S(2)}) copy-start(f32[32,1,16,128]{3,2,0,1:T(8,128)} %get-tuple-element.46) | copy-start | bytes 786436
  385.2 93.0 %copy-start.8 = (f32[32,1,16,128]{3,2,0,1:T(8,128)S(1)}, f32[32,1,16,128]{3,2,0,1:T(8,128)}, u32[]{:S(2)}) copy-start(f32[32,1,16,128]{3,2,0,1:T(8,128)} %get-tuple-element.47) | copy-start | bytes 786436
  385.2 93.0 %copy-start.9 = (f32[32,1,16,128]{3,2,0,1:T(8,128)S(1)}, f32[32,1,16,128]{3,2,0,1:T(8,128)}, u32[]{:S(2)}) copy-start(f32[32,1,16,128]{3,2,0,1:T(8,128)} %get-tuple-element.42) | copy-start | bytes 786436
  385.2 93.0 %copy-start.10 = (f32[32,1,16,128]{3,2,0,1:T(8,128)S(1)}, f32[32,1,16,128]{3,2,0,1:T(8,128)}, u32[]{:S(2)}) copy-start(f32[32,1,16,128]{3,2,0,1:T(8,128)} %get-tuple-element.43) | copy-start | bytes 786436
  385.2 93.0 %copy-start.11 = (f32[32,1,16,128]{3,2,0,1:T(8,128)S(1)}, f32[32,1,16,128]{3,2,0,1:T(8,128)}, u32[]{:S(2)}) copy-start(f32[32,1,16,128]{3,2,0,1:T(8,128)} %get-tuple-element.38) | copy-start | bytes 786436
  385.3 93.0 %copy-start.12 = (f32[32,1,16,128]{3,2,0,1:T(8,128)S(1)}, f32[32,1,16,128]{3,2,0,1:T(8,128)}, u32[]{:S(2)}) copy-start(f32[32,1,16,128]{3,2,0,1:T(8,128)} %get-tuple-element.39) | copy-start | bytes 786436
  385.3 93.0 %copy-start.13 = (f32[32,1,16,128]{3,2,0,1:T(8,128)S(1)}, f32[32,1,16,128]{3,2,0,1:T(8,128)}, u32[]{:S(2)}) copy-start(f32[32,1,16,128]{3,2,0,1:T(8,128)} %get-tuple-element.34) | copy-start | bytes 786436
  385.3 93.0 %copy-start.14 = (f32[32,1,16,128]{3,2,0,1:T(8,128)S(1)}, f32[32,1,16,128]{3,2,0,1:T(8,128)}, u32[]{:S(2)}) copy-start(f32[32,1,16,128]{3,2,0,1:T(8,128)} %get-tuple-element.35) | copy-start | bytes 786436
where the time goes:
time: 483 us
  blocking collectives  166 us (34%)
  starting transfers between devices  157 us (33%)
  waiting for transfers between devices  92.4 us (19%)
  matrix products  29.5 us (6%)
  other arithmetic  23 us (5%)
  between operations  9.08 us (2%)
  local copies, waits for them, and re-layouts  5.74 us (1%)
    psum x1, blocking collectives, shards(): misfit_total = lax.psum(misfit_sum, ('chan', 'freq'))  166 us
    ppermute x16, starting transfers between devices, shifted(): return lax.ppermute(x, axis, [(i, (i + by) % peers) for i in range(peers)])  157 us
    ppermute x16, waiting for transfers between devices, shifted(): return lax.ppermute(x, axis, [(i, (i + by) % peers) for i in range(peers)])  92.4 us
    dot_general x9, matrix products, pair_terms(): jnp.einsum('xfrc,frd->xfcd', stacked_left, right_rows, preferred_element_...  17.4 us
  transfers between devices with their start and end apart: 16, of which 3 were waited for; matrix products, arithmetic and copies ran while one was open for 11% of the time, Pallas kernels for 0%

commit v1 on v0

--- a/solution.py
+++ b/solution.py
@@ -79,7 +79,7 @@
         misfit_sum = misfit_sum + piece_loss
         adjoint_acc = adjoint_acc + near_terms
         adjoint_acc = adjoint_acc + shifted(far_terms, "chan", s)
-    misfit_total = lax.psum(misfit_sum, ("chan", "freq"))
+    misfit_total = jnp.sum(lax.all_gather(misfit_sum, ("chan", "freq")), axis=0)
     misfit = misfit_total / float(F * block_width * block_total * BAND)
     return (adjoint_acc * (1.0 / W), misfit)
 

time: 483 us -> 495 us (1.025)
  the two profiles are of different devices: /device:TPU:104 before, /device:TPU:192 now
where the time goes in v1:
time: 495 us; the launch traced here: 494 us
  waiting for transfers between devices  190 us (38%)
  starting transfers between devices  115 us (23%)
  blocking collectives  115 us (23%)
  matrix products  29.5 us (6%)
  other arithmetic  25.6 us (5%)
  local copies, waits for them, and re-layouts  9.82 us (2%)
  between operations  9.13 us (2%)
    ppermute x16, waiting for transfers between devices, shifted(): return lax.ppermute(x, axis, [(i, (i + by) % peers) for i in range(peers)])  190 us
    ppermute x16, starting transfers between devices, shifted(): return lax.ppermute(x, axis, [(i, (i + by) % peers) for i in range(peers)])  115 us
    unnamed x1, blocking collectives  115 us
    dot_general x9, matrix products, pair_terms(): jnp.einsum('xfrc,frd->xfcd', stacked_left, right_rows, preferred_element_...  17.4 us
  transfers between devices with their start and end apart: 16, of which 5 were waited for; matrix products, arithmetic and copies ran while one was open for 12% of the time, Pallas kernels for 0%

profile of v1, /device:TPU:192, one launch (start us, length us, event | category | flops | bytes accessed | tf_op | source)
XLA Modules:
  0.0 493.8 jit_solution(9536088443471651797)
XLA Ops:
  0.7 1.0 constant_dynamic-update-slice_fusion.1
  1.6 0.9 constant_dynamic-update-slice_fusion
  2.6 1.4 broadcast_multiply_fusion
  4.0 7.4 %collective-permute-start.14 = (bf16[32,2,24,128]{3,2,0,1:T(8,128)(2,1)}, bf16[32,2,24,128]{3,2,0,1:T(8,128)(2,1)}, u32[]{:S(2)}, u32[]{:S(2)}) collective-permute-start(bf16[32,2,24,128]{3,2,0,1:T(8,128)(2,1)} %get-tuple-element.61), channel_id=1, source_target_pairs={{0,448},{8,456},{16,464},{24,472},{32,480},{40,488},{48,496},{56,5... | collective-permute-start | bytes 1179656 | tf_op jit(solution)/shard_map/ppermute | solution.py:13
  11.4 1.9 collective-permute-start.12
  13.3 11.4 %collective-permute-start.10 = (bf16[32,2,24,128]{3,2,0,1:T(8,128)(2,1)}, bf16[32,2,24,128]{3,2,0,1:T(8,128)(2,1)S(1)}, u32[]{:S(2)}, u32[]{:S(2)}) collective-permute-start(bf16[32,2,24,128]{3,2,0,1:T(8,128)(2,1)} %get-tuple-element.61), channel_id=1, source_target_pairs={{0,464},{8,472},{16,480},{24,488},{32,496},{40,504},{48,0},{56,8},... | collective-permute-start | bytes 1179656 | tf_op jit(solution)/shard_map/ppermute | solution.py:13
  24.8 12.3 %collective-permute-start.8 = (bf16[32,2,24,128]{3,2,0,1:T(8,128)(2,1)}, bf16[32,2,24,128]{3,2,0,1:T(8,128)(2,1)S(1)}, u32[]{:S(2)}, u32[]{:S(2)}) collective-permute-start(bf16[32,2,24,128]{3,2,0,1:T(8,128)(2,1)} %get-tuple-element.61), channel_id=1, source_target_pairs={{0,472},{8,480},{16,488},{24,496},{32,504},{40,0},{48,8},{56,16},{... | collective-permute-start | bytes 1179656 | tf_op jit(solution)/shard_map/ppermute | solution.py:13
  37.1 3.0 collective-permute-start.6
  41.4 1.8 multiply_select_fusion.8
  43.2 2.0 multiply_reduce_fusion.8
  45.2 0.8 fusion.91
  47.9 0.9 fusion.144
  48.7 1.9 collective-permute-start.4
  50.7 1.0 copy.99
  51.7 1.9 multiply_reduce_fusion
  53.6 0.8 fusion.88
  54.4 1.0 slice.417
  56.0 0.9 fusion.114
  56.8 39.9 %collective-permute-done.12 = bf16[32,2,24,128]{3,2,0,1:T(8,128)(2,1)} collective-permute-done((bf16[32,2,24,128]{3,2,0,1:T(8,128)(2,1)}, bf16[32,2,24,128]{3,2,0,1:T(8,128)(2,1)}, u32[]{:S(2)}, u32[]{:S(2)}) %collective-permute-start.12) | collective-permute-done | bytes 393248 | tf_op jit(solution)/shard_map/ppermute | solution.py:13
  96.8 1.9 collective-permute-start.2
  98.7 1.0 copy.93
  99.7 2.0 multiply_reduce_fusion.1
  102.5 1.0 slice.408
  104.0 0.9 fusion.118
  104.9 37.2 %collective-permute-start = (bf16[32,2,24,128]{3,2,0,1:T(8,128)(2,1)}, bf16[32,2,24,128]{3,2,0,1:T(8,128)(2,1)S(1)}, u32[]{:S(2)}, u32[]{:S(2)}) collective-permute-start(bf16[32,2,24,128]{3,2,0,1:T(8,128)(2,1)} %get-tuple-element.61), channel_id=1, source_target_pairs={{0,504},{8,0},{16,8},{24,16},{32,24},{40,32},{48,40},{56,48},{64,5... | collective-permute-start | bytes 1179656 | tf_op jit(solution)/shard_map/ppermute | solution.py:13
  142.1 2.0 multiply_reduce_fusion.2
  144.1 0.8 fusion.76
  145.5 0.8 pad_maximum_fusion.8
  147.1 57.2 %collective-permute-done.8 = bf16[32,2,24,128]{3,2,0,1:T(8,128)(2,1)S(1)} collective-permute-done((bf16[32,2,24,128]{3,2,0,1:T(8,128)(2,1)}, bf16[32,2,24,128]{3,2,0,1:T(8,128)(2,1)S(1)}, u32[]{:S(2)}, u32[]{:S(2)}) %collective-permute-start.8) | collective-permute-done | bytes 393248 | tf_op jit(solution)/shard_map/ppermute | solution.py:13
  204.3 2.1 collective-permute-start.15
  206.5 2.0 multiply_reduce_fusion.3
  208.5 0.8 fusion.70
  209.8 0.8 pad_maximum_fusion.7
  211.5 1.9 collective-permute-start.13
  213.4 1.9 multiply_reduce_fusion.4
  215.3 0.8 fusion.64
  216.7 0.9 pad_maximum_fusion.6
  218.3 16.0 %collective-permute-start.11 = (f32[32,2,16,128]{3,2,0,1:T(8,128)}, f32[32,2,16,128]{3,2,0,1:T(8,128)}, u32[]{:S(2)}, u32[]{:S(2)}) collective-permute-start(f32[32,2,16,128]{3,2,0,1:T(8,128)} %pad_maximum_fusion.6), channel_id=1, source_target_pairs={{0,48},{8,56},{16,64},{24,72},{32,80},{40,88},{48,96},{56,104},{64... | collective-permute-start | bytes 1572872 | tf_op jit(solution)/shard_map/ppermute | solution.py:13
  234.4 1.9 multiply_reduce_fusion.5
  236.3 0.8 fusion.58
  237.2 0.9 fusion.132
  238.1 0.8 pad_maximum_fusion.5
  239.4 1.9 collective-permute-start.9
  241.4 1.9 multiply_reduce_fusion.6
  244.1 0.9 fusion.134
  245.7 0.8 pad_maximum_fusion.4
  246.5 0.9 fusion.136
  247.5 1.9 collective-permute-start.7
  249.4 1.9 multiply_reduce_fusion.7
  251.3 0.8 fusion.46
  252.1 0.9 fusion.140
  259.6 114.6 %all-reduce = f32[512]{0:T(512)S(1)} all-reduce(f32[512]{0:T(512)S(1)} %dynamic-update-slice), channel_id=1, replica_groups=mesh['chan'=64,'freq'=8] {'chan','freq'}, use_global_device_ids=true, to_apply=%add | all-reduce | flops 512 | bytes 4096
  374.7 1.8 pad_maximum_fusion.3
  376.6 1.9 pad_maximum_fusion.2
  378.5 0.9 pad_maximum_fusion.1
  380.1 1.5 fusion.49
  381.7 4.4 collective-permute-start.5
  386.1 8.1 %collective-permute-start.3 = (f32[32,2,16,128]{3,2,0,1:T(8,128)S(1)}, f32[32,2,16,128]{3,2,0,1:T(8,128)S(1)}, u32[]{:S(2)}, u32[]{:S(2)}) collective-permute-start(f32[32,2,16,128]{3,2,0,1:T(8,128)S(1)} %copy-done.21), channel_id=1, source_target_pairs={{0,16},{8,24},{16,32},{24,40},{32,48},{40,56},{48,64},{56,72},{64,... | collective-permute-start | bytes 1572872 | tf_op jit(solution)/shard_map/ppermute | solution.py:13
  394.2 1.9 collective-permute-start.1
  396.8 23.7 %collective-permute-done.5 = f32[32,2,16,128]{3,2,0,1:T(8,128)S(1)} collective-permute-done((f32[32,2,16,128]{3,2,0,1:T(8,128)S(1)}, f32[32,2,16,128]{3,2,0,1:T(8,128)S(1)}, u32[]{:S(2)}, u32[]{:S(2)}) %collective-permute-start.5) | collective-permute-done | bytes 524320 | tf_op jit(solution)/shard_map/ppermute | solution.py:13
  420.5 67.7 %collective-permute-done.3 = f32[32,2,16,128]{3,2,0,1:T(8,128)S(1)} collective-permute-done((f32[32,2,16,128]{3,2,0,1:T(8,128)S(1)}, f32[32,2,16,128]{3,2,0,1:T(8,128)S(1)}, u32[]{:S(2)}, u32[]{:S(2)}) %collective-permute-start.3) | collective-permute-done | bytes 524320 | tf_op jit(solution)/shard_map/ppermute | solution.py:13
  488.2 1.2 collective-permute-done.1
  489.5 2.3 fusion.110
  491.8 0.9 copy.104
  (144 shorter events, 13.0 us)
Async XLA Ops:
  0.6 39.8 %copy-start.36 = (bf16[24]{0:T(256)(128)(2,1)S(1)}, bf16[24]{0:T(256)(128)(2,1)}, u32[]{:S(2)}) copy-start(bf16[24]{0:T(256)(128)(2,1)} %constant.88.clone.1) | copy-start | bytes 148
  0.6 39.7 %copy-start.35 = (s32[8192]{0:T(1024)S(1)}, s32[8192]{0:T(1024)}, u32[]{:S(2)}) copy-start(s32[8192]{0:T(1024)} %param.6) | copy-start | bytes 98308
  0.7 39.8 %copy-start.37 = (s32[64]{0:T(128)S(1)}, s32[64]{0:T(128)}, u32[]{:S(2)}) copy-start(s32[64]{0:T(128)} %param.7) | copy-start | bytes 772
  4.0 44.7 %collective-permute-start.14 = (bf16[32,2,24,128]{3,2,0,1:T(8,128)(2,1)}, bf16[32,2,24,128]{3,2,0,1:T(8,128)(2,1)}, u32[]{:S(2)}, u32[]{:S(2)}) collective-permute-start(bf16[32,2,24,128]{3,2,0,1:T(8,128)(2,1)} %get-tuple-element.61), channel_id=1, source_target_pairs={{0,448},{8,456},{16,464},{24,472},{32,480},{40,488},{48,496},{56,5... | collective-permute-start | bytes 1179656 | tf_op jit(solution)/shard_map/ppermute | solution.py:13
  11.4 85.4 %collective-permute-start.12 = (bf16[32,2,24,128]{3,2,0,1:T(8,128)(2,1)}, bf16[32,2,24,128]{3,2,0,1:T(8,128)(2,1)}, u32[]{:S(2)}, u32[]{:S(2)}) collective-permute-start(bf16[32,2,24,128]{3,2,0,1:T(8,128)(2,1)} %get-tuple-element.61), channel_id=1, source_target_pairs={{0,456},{8,464},{16,472},{24,480},{32,488},{40,496},{48,504},{56,0... | collective-permute-start | bytes 1179656 | tf_op jit(solution)/shard_map/ppermute | solution.py:13
  13.3 91.6 %collective-permute-start.10 = (bf16[32,2,24,128]{3,2,0,1:T(8,128)(2,1)}, bf16[32,2,24,128]{3,2,0,1:T(8,128)(2,1)S(1)}, u32[]{:S(2)}, u32[]{:S(2)}) collective-permute-start(bf16[32,2,24,128]{3,2,0,1:T(8,128)(2,1)} %get-tuple-element.61), channel_id=1, source_target_pairs={{0,464},{8,472},{16,480},{24,488},{32,496},{40,504},{48,0},{56,8},... | collective-permute-start | bytes 1179656 | tf_op jit(solution)/shard_map/ppermute | solution.py:13
  24.8 179.6 %collective-permute-start.8 = (bf16[32,2,24,128]{3,2,0,1:T(8,128)(2,1)}, bf16[32,2,24,128]{3,2,0,1:T(8,128)(2,1)S(1)}, u32[]{:S(2)}, u32[]{:S(2)}) collective-permute-start(bf16[32,2,24,128]{3,2,0,1:T(8,128)(2,1)} %get-tuple-element.61), channel_id=1, source_target_pairs={{0,472},{8,480},{16,488},{24,496},{32,504},{40,0},{48,8},{56,16},{... | collective-permute-start | bytes 1179656 | tf_op jit(solution)/shard_map/ppermute | solution.py:13
  37.1 174.4 %collective-permute-start.6 = (bf16[32,2,24,128]{3,2,0,1:T(8,128)(2,1)}, bf16[32,2,24,128]{3,2,0,1:T(8,128)(2,1)S(1)}, u32[]{:S(2)}, u32[]{:S(2)}) collective-permute-start(bf16[32,2,24,128]{3,2,0,1:T(8,128)(2,1)} %get-tuple-element.61), channel_id=1, source_target_pairs={{0,480},{8,488},{16,496},{24,504},{32,0},{40,8},{48,16},{56,24},{6... | collective-permute-start | bytes 1179656 | tf_op jit(solution)/shard_map/ppermute | solution.py:13
  41.1 4.0 copy-start.23
  41.2 3.9 copy-start.25
  43.2 2.0 copy-start
  47.2 4.6 copy-start.24
  47.2 4.6 copy-start.26
  47.2 4.6 copy-start.34
  48.7 169.6 %collective-permute-start.4 = (bf16[32,2,24,128]{3,2,0,1:T(8,128)(2,1)}, bf16[32,2,24,128]{3,2,0,1:T(8,128)(2,1)S(1)}, u32[]{:S(2)}, u32[]{:S(2)}) collective-permute-start(bf16[32,2,24,128]{3,2,0,1:T(8,128)(2,1)} %get-tuple-element.61), channel_id=1, source_target_pairs={{0,488},{8,496},{16,504},{24,0},{32,8},{40,16},{48,24},{56,32},{64... | collective-permute-start | bytes 1179656 | tf_op jit(solution)/shard_map/ppermute | solution.py:13
  55.9 43.9 %copy-start.33 = (f32[128,128]{0,1:T(8,128)S(1)}, f32[128,128]{0,1:T(8,128)}, u32[]{:S(2)}) copy-start(f32[128,128]{0,1:T(8,128)} %get-tuple-element.77) | copy-start | bytes 196612
  96.8 142.6 %collective-permute-start.2 = (bf16[32,2,24,128]{3,2,0,1:T(8,128)(2,1)}, bf16[32,2,24,128]{3,2,0,1:T(8,128)(2,1)S(1)}, u32[]{:S(2)}, u32[]{:S(2)}) collective-permute-start(bf16[32,2,24,128]{3,2,0,1:T(8,128)(2,1)} %get-tuple-element.61), channel_id=1, source_target_pairs={{0,496},{8,504},{16,0},{24,8},{32,16},{40,24},{48,32},{56,40},{64,... | collective-permute-start | bytes 1179656 | tf_op jit(solution)/shard_map/ppermute | solution.py:13
  103.9 38.2 %copy-start.32 = (f32[128,128]{0,1:T(8,128)S(1)}, f32[128,128]{0,1:T(8,128)}, u32[]{:S(2)}) copy-start(f32[128,128]{0,1:T(8,128)} %get-tuple-element.76) | copy-start | bytes 196612
  104.9 142.6 %collective-permute-start = (bf16[32,2,24,128]{3,2,0,1:T(8,128)(2,1)}, bf16[32,2,24,128]{3,2,0,1:T(8,128)(2,1)S(1)}, u32[]{:S(2)}, u32[]{:S(2)}) collective-permute-start(bf16[32,2,24,128]{3,2,0,1:T(8,128)(2,1)} %get-tuple-element.61), channel_id=1, source_target_pairs={{0,504},{8,0},{16,8},{24,16},{32,24},{40,32},{48,40},{56,48},{64,5... | collective-permute-start | bytes 1179656 | tf_op jit(solution)/shard_map/ppermute | solution.py:13
  145.5 61.0 %copy-start.31 = (f32[128,128]{0,1:T(8,128)S(1)}, f32[128,128]{0,1:T(8,128)}, u32[]{:S(2)}) copy-start(f32[128,128]{0,1:T(8,128)} %get-tuple-element.75) | copy-start | bytes 196612
  204.3 177.3 %collective-permute-start.15 = (f32[32,2,16,128]{3,2,0,1:T(8,128)}, f32[32,2,16,128]{3,2,0,1:T(8,128)}, u32[]{:S(2)}, u32[]{:S(2)}) collective-permute-start(f32[32,2,16,128]{3,2,0,1:T(8,128)} %pad_maximum_fusion.8), channel_id=1, source_target_pairs={{0,64},{8,72},{16,80},{24,88},{32,96},{40,104},{48,112},{56,120},{... | collective-permute-start | bytes 1572872 | tf_op jit(solution)/shard_map/ppermute | solution.py:13
  209.8 3.6 copy-start.30
  211.5 174.6 %collective-permute-start.13 = (f32[32,2,16,128]{3,2,0,1:T(8,128)}, f32[32,2,16,128]{3,2,0,1:T(8,128)}, u32[]{:S(2)}, u32[]{:S(2)}) collective-permute-start(f32[32,2,16,128]{3,2,0,1:T(8,128)} %pad_maximum_fusion.7), channel_id=1, source_target_pairs={{0,56},{8,64},{16,72},{24,80},{32,88},{40,96},{48,104},{56,112},{6... | collective-permute-start | bytes 1572872 | tf_op jit(solution)/shard_map/ppermute | solution.py:13
  216.7 17.7 %copy-start.29 = (f32[128,128]{0,1:T(8,128)S(1)}, f32[128,128]{0,1:T(8,128)}, u32[]{:S(2)}) copy-start(f32[128,128]{0,1:T(8,128)} %get-tuple-element.73) | copy-start | bytes 196612
  218.3 175.9 %collective-permute-start.11 = (f32[32,2,16,128]{3,2,0,1:T(8,128)}, f32[32,2,16,128]{3,2,0,1:T(8,128)}, u32[]{:S(2)}, u32[]{:S(2)}) collective-permute-start(f32[32,2,16,128]{3,2,0,1:T(8,128)} %pad_maximum_fusion.6), channel_id=1, source_target_pairs={{0,48},{8,56},{16,64},{24,72},{32,80},{40,88},{48,96},{56,104},{64... | collective-permute-start | bytes 1572872 | tf_op jit(solution)/shard_map/ppermute | solution.py:13
  239.0 2.4 copy-start.28
  239.4 157.4 %collective-permute-start.9 = (f32[32,2,16,128]{3,2,0,1:T(8,128)}, f32[32,2,16,128]{3,2,0,1:T(8,128)}, u32[]{:S(2)}, u32[]{:S(2)}) collective-permute-start(f32[32,2,16,128]{3,2,0,1:T(8,128)} %pad_maximum_fusion.5), channel_id=1, source_target_pairs={{0,40},{8,48},{16,56},{24,64},{32,72},{40,80},{48,88},{56,96},{64,... | collective-permute-start | bytes 1572872 | tf_op jit(solution)/shard_map/ppermute | solution.py:13
  245.0 4.5 copy-start.27
  247.5 149.3 %collective-permute-start.7 = (f32[32,2,16,128]{3,2,0,1:T(8,128)}, f32[32,2,16,128]{3,2,0,1:T(8,128)}, u32[]{:S(2)}, u32[]{:S(2)}) collective-permute-start(f32[32,2,16,128]{3,2,0,1:T(8,128)} %pad_maximum_fusion.4), channel_id=1, source_target_pairs={{0,32},{8,40},{16,48},{24,56},{32,64},{40,72},{48,80},{56,88},{64,... | collective-permute-start | bytes 1572872 | tf_op jit(solution)/shard_map/ppermute | solution.py:13
  251.3 1.7 copy-start.1
  252.1 122.6 %copy-start.16 = (f32[32,1,16,128]{3,2,0,1:T(8,128)S(1)}, f32[32,1,16,128]{3,2,0,1:T(8,128)}, u32[]{:S(2)}) copy-start(f32[32,1,16,128]{3,2,0,1:T(8,128)} %get-tuple-element.36) | copy-start | bytes 786436
  374.7 3.7 copy-start.17
  374.7 3.7 copy-start.18
  380.0 1.6 copy-start.20
  380.0 6.1 %copy-start.21 = (f32[32,2,16,128]{3,2,0,1:T(8,128)S(1)}, f32[32,2,16,128]{3,2,0,1:T(8,128)}, u32[]{:S(2)}) copy-start(f32[32,2,16,128]{3,2,0,1:T(8,128)} %pad_maximum_fusion.2) | copy-start | bytes 1572868
  380.0 14.2 %copy-start.22 = (f32[32,2,16,128]{3,2,0,1:T(8,128)S(1)}, f32[32,2,16,128]{3,2,0,1:T(8,128)}, u32[]{:S(2)}) copy-start(f32[32,2,16,128]{3,2,0,1:T(8,128)} %pad_maximum_fusion.1) | copy-start | bytes 1572868
  380.0 16.1 %copy-start.2 = (bf16[2,32,128,128]{2,3,0,1:T(8,128)(2,1)S(1)}, bf16[2,32,128,128]{2,3,0,1:T(8,128)(2,1)}, u32[]{:S(2)}) copy-start(bf16[2,32,128,128]{2,3,0,1:T(8,128)(2,1)} %copy-done.1) | copy-start | bytes 6291460
  380.1 16.1 %copy-start.19 = (bf16[32,2,16,128]{3,2,1,0:T(8,128)(2,1)S(1)}, bf16[32,2,16,128]{3,2,1,0:T(8,128)(2,1)}, u32[]{:S(2)}) copy-start(bf16[32,2,16,128]{3,2,1,0:T(8,128)(2,1)} %copy.56) | copy-start | bytes 786436
  381.7 38.9 %collective-permute-start.5 = (f32[32,2,16,128]{3,2,0,1:T(8,128)S(1)}, f32[32,2,16,128]{3,2,0,1:T(8,128)S(1)}, u32[]{:S(2)}, u32[]{:S(2)}) collective-permute-start(f32[32,2,16,128]{3,2,0,1:T(8,128)S(1)} %copy-done.20), channel_id=1, source_target_pairs={{0,24},{8,32},{16,40},{24,48},{32,56},{40,64},{48,72},{56,80},{64,... | collective-permute-start | bytes 1572872 | tf_op jit(solution)/shard_map/ppermute | solution.py:13
  386.1 102.1 %collective-permute-start.3 = (f32[32,2,16,128]{3,2,0,1:T(8,128)S(1)}, f32[32,2,16,128]{3,2,0,1:T(8,128)S(1)}, u32[]{:S(2)}, u32[]{:S(2)}) collective-permute-start(f32[32,2,16,128]{3,2,0,1:T(8,128)S(1)} %copy-done.21), channel_id=1, source_target_pairs={{0,16},{8,24},{16,32},{24,40},{32,48},{40,56},{48,64},{56,72},{64,... | collective-permute-start | bytes 1572872 | tf_op jit(solution)/shard_map/ppermute | solution.py:13
  394.2 95.2 %collective-permute-start.1 = (f32[32,2,16,128]{3,2,0,1:T(8,128)S(1)}, f32[32,2,16,128]{3,2,0,1:T(8,128)S(1)}, u32[]{:S(2)}, u32[]{:S(2)}) collective-permute-start(f32[32,2,16,128]{3,2,0,1:T(8,128)S(1)} %copy-done.22), channel_id=1, source_target_pairs={{0,8},{8,16},{16,24},{24,32},{32,40},{40,48},{48,56},{56,64},{64,7... | collective-permute-start | bytes 1572872 | tf_op jit(solution)/shard_map/ppermute | solution.py:13
  396.2 93.3 %copy-start.3 = (f32[32,1,16,128]{3,2,0,1:T(8,128)S(1)}, f32[32,1,16,128]{3,2,0,1:T(8,128)}, u32[]{:S(2)}) copy-start(f32[32,1,16,128]{3,2,0,1:T(8,128)} %fusion.145) | copy-start | bytes 786436
  396.2 93.2 %copy-start.4 = (f32[32,1,16,128]{3,2,0,1:T(8,128)S(1)}, f32[32,1,16,128]{3,2,0,1:T(8,128)}, u32[]{:S(2)}) copy-start(f32[32,1,16,128]{3,2,0,1:T(8,128)} %fusion.147) | copy-start | bytes 786436
  396.2 93.2 %copy-start.5 = (f32[32,1,16,128]{3,2,0,1:T(8,128)S(1)}, f32[32,1,16,128]{3,2,0,1:T(8,128)}, u32[]{:S(2)}) copy-start(f32[32,1,16,128]{3,2,0,1:T(8,128)} %get-tuple-element.24) | copy-start | bytes 786436
  396.2 93.2 %copy-start.6 = (f32[32,1,16,128]{3,2,0,1:T(8,128)S(1)}, f32[32,1,16,128]{3,2,0,1:T(8,128)}, u32[]{:S(2)}) copy-start(f32[32,1,16,128]{3,2,0,1:T(8,128)} %get-tuple-element.25) | copy-start | bytes 786436
  396.2 93.2 %copy-start.7 = (f32[32,1,16,128]{3,2,0,1:T(8,128)S(1)}, f32[32,1,16,128]{3,2,0,1:T(8,128)}, u32[]{:S(2)}) copy-start(f32[32,1,16,128]{3,2,0,1:T(8,128)} %get-tuple-element.54) | copy-start | bytes 786436
  396.2 93.2 %copy-start.8 = (f32[32,1,16,128]{3,2,0,1:T(8,128)S(1)}, f32[32,1,16,128]{3,2,0,1:T(8,128)}, u32[]{:S(2)}) copy-start(f32[32,1,16,128]{3,2,0,1:T(8,128)} %get-tuple-element.55) | copy-start | bytes 786436
  396.2 93.2 %copy-start.9 = (f32[32,1,16,128]{3,2,0,1:T(8,128)S(1)}, f32[32,1,16,128]{3,2,0,1:T(8,128)}, u32[]{:S(2)}) copy-start(f32[32,1,16,128]{3,2,0,1:T(8,128)} %get-tuple-element.50) | copy-start | bytes 786436
  396.2 93.2 %copy-start.10 = (f32[32,1,16,128]{3,2,0,1:T(8,128)S(1)}, f32[32,1,16,128]{3,2,0,1:T(8,128)}, u32[]{:S(2)}) copy-start(f32[32,1,16,128]{3,2,0,1:T(8,128)} %get-tuple-element.51) | copy-start | bytes 786436
  396.2 93.2 %copy-start.11 = (f32[32,1,16,128]{3,2,0,1:T(8,128)S(1)}, f32[32,1,16,128]{3,2,0,1:T(8,128)}, u32[]{:S(2)}) copy-start(f32[32,1,16,128]{3,2,0,1:T(8,128)} %get-tuple-element.47) | copy-start | bytes 786436
  396.2 93.2 %copy-start.12 = (f32[32,1,16,128]{3,2,0,1:T(8,128)S(1)}, f32[32,1,16,128]{3,2,0,1:T(8,128)}, u32[]{:S(2)}) copy-start(f32[32,1,16,128]{3,2,0,1:T(8,128)} %get-tuple-element.43) | copy-start | bytes 786436
  396.3 93.2 %copy-start.13 = (f32[32,1,16,128]{3,2,0,1:T(8,128)S(1)}, f32[32,1,16,128]{3,2,0,1:T(8,128)}, u32[]{:S(2)}) copy-start(f32[32,1,16,128]{3,2,0,1:T(8,128)} %get-tuple-element.39) | copy-start | bytes 786436
  396.3 93.2 %copy-start.14 = (f32[32,1,16,128]{3,2,0,1:T(8,128)S(1)}, f32[32,1,16,128]{3,2,0,1:T(8,128)}, u32[]{:S(2)}) copy-start(f32[32,1,16,128]{3,2,0,1:T(8,128)} %get-tuple-element.34) | copy-start | bytes 786436
  396.3 93.2 %copy-start.15 = (f32[32,1,16,128]{3,2,0,1:T(8,128)S(1)}, f32[32,1,16,128]{3,2,0,1:T(8,128)}, u32[]{:S(2)}) copy-start(f32[32,1,16,128]{3,2,0,1:T(8,128)} %get-tuple-element.35) | copy-start | bytes 786436
